TPU v7x, 512 devices: a whole 4x4x16 slice. The times are simulated.
512 devices in a mesh: row: 32 (over z, core), col: 16 (over x, y).
Axes of the slice: x: 4, y: 4, z: 16, core: 2. Of those that a mesh axis runs over, the one named last changes fastest.
Arguments:
- weight: bfloat16 [8192, 53248], P('row', 'col'), may hold values from -6 to 6
- inverse_rows: float32 [512, 53248], P('row', 'col'), as said below
- pruned_index: int32 [512], replicated, may hold values from 0 to 53247, as said below
Outputs:
- pruned_weight: bfloat16 [8192, 53248], P('row', 'col')
- saliency: float32 [8192], P('row')
Inputs may be any that keep to these rules, and one draw needn't show every extreme that they name: `pruned_index`: distinct and ascending. Neuron c lies in column shard c // 3328; at most 96 of them lie in one shard, and exactly 96 in one shard. `inverse_rows`: its columns pruned_index form a symmetric positive definite matrix.
All inputs are finite; a program needn't handle non-finite values.
Results may differ from a plain program's by a relative error of at most 0.001.
Values may be sent and summed in bfloat16 or wider, within the bound.
A program may use at most 64 MiB of HBM per device.

v0:
```python
import jax
import jax.numpy as jnp
from jax import lax
from jax.sharding import Mesh
from jax.sharding import PartitionSpec as P

ROW = ("row_0", "row_1")


def from_everyone(value, axis):
    count = lax.axis_size(axis)
    return lax.all_to_all(
        jnp.broadcast_to(value[None], (count, *value.shape)), axis, 0, 0, tiled=True
    )


def joined_along(parts, dim):
    parts = jnp.moveaxis(parts, 0, dim)
    shape = parts.shape
    return parts.reshape(*shape[:dim], shape[dim] * shape[dim + 1], *shape[dim + 2 :])


def gather_directly(value, axis, dim):
    parts = from_everyone(value, axis)
    return joined_along(parts, dim)


def all_blocks(value, axes, sequence):
    parts = value[None]
    for k in sequence:
        parts = lax.all_gather(parts, axes[k], axis=0, tiled=True)
    carried = [lax.axis_size(axes[k]) for k in reversed(sequence)]
    parts = parts.reshape(*carried, *value.shape)
    turned = sorted(range(len(sequence)), key=lambda place: sequence[len(sequence) - 1 - place])
    return parts.transpose(*turned, *range(len(sequence), parts.ndim)).reshape(-1, *value.shape)


def whole_of(value, axes, sequence, dim):
    return joined_along(all_blocks(value, axes, sequence), dim)


def body(weight, inverse_rows, pruned_index):
    row_count, col_width = weight.shape
    pruned_count = pruned_index.shape[0]
    col_devices = lax.axis_size("col")
    own_index = lax.axis_index("col")
    col_anchor = own_index * col_width
    capacity = 3 * pruned_count // col_devices
    boundary = jnp.arange(col_devices + 1, dtype=jnp.int32) * col_width
    edges_at = jnp.sum((pruned_index[None, :] < boundary[:, None]).astype(jnp.int32), axis=1)
    starts = edges_at[:-1]
    counts = edges_at[1:] - edges_at[:-1]
    window_start = starts[own_index]
    padded = jnp.concatenate([pruned_index, jnp.full((capacity,), -1, jnp.int32)])
    window = lax.dynamic_slice_in_dim(padded, window_start, capacity) - col_anchor
    slot_ids = jnp.arange(capacity, dtype=jnp.int32)
    occupied = slot_ids < counts[own_index]
    clipped = jnp.clip(window, 0, col_width - 1)
    column_ids = lax.broadcasted_iota(jnp.int32, (col_width, capacity), 0)
    picker = ((column_ids == clipped[None, :]) & occupied[None, :]).astype(jnp.bfloat16)
    weight_window = jnp.dot(weight, picker, preferred_element_type=jnp.float32).astype(jnp.bfloat16)
    inverse_window = jnp.where(occupied[None, :], jnp.take(inverse_rows, clipped, axis=1), 0.0)
    weight_all = gather_directly(weight_window, "col", 1)
    inverse_all = gather_directly(inverse_window, "col", 1)
    targets = (starts[:, None] + slot_ids[None, :]).reshape(-1)
    is_valid = (slot_ids[None, :] < counts[:, None]).reshape(-1)
    neuron_ids = lax.broadcasted_iota(jnp.int32, (col_devices * capacity, pruned_count), 1)
    placer = (neuron_ids == targets[:, None]) & is_valid[:, None]
    weight_pruned = jnp.dot(
        weight_all, placer.astype(jnp.bfloat16), preferred_element_type=jnp.float32
    )
    schur_part = jnp.dot(
        inverse_all,
        placer.astype(jnp.float32),
        precision=lax.Precision.HIGHEST,
        preferred_element_type=jnp.float32,
    )
    schur_block = whole_of(schur_part, ROW, (0, 1), 0)
    factor_low = jnp.linalg.cholesky(schur_block)
    solved = jax.scipy.linalg.cho_solve((factor_low, True), weight_pruned.T).T
    correction = jnp.dot(
        solved,
        lax.all_gather(inverse_rows, ROW, axis=0, tiled=True),
        precision=lax.Precision.HIGHEST,
        preferred_element_type=jnp.float32,
    )
    pruned_weight = (weight.astype(jnp.float32) - correction).astype(jnp.bfloat16)
    saliency = jnp.sum(solved * weight_pruned, axis=1) / (2.0 * pruned_count)
    return (pruned_weight, saliency)


def solution(mesh):
    split = Mesh(mesh.devices.reshape(16, 2, mesh.shape["col"]), ("row_0", "row_1", "col"))
    return jax.shard_map(
        body,
        mesh=split,
        in_specs=(P(ROW, "col"), P(ROW, "col"), P()),
        out_specs=(P(ROW, "col"), P(ROW)),
        check_vma=False,
    )
```

profile of v0, /device:TPU:8, one launch (start us, length us, event | category | flops | bytes accessed | tf_op | source)
XLA Modules:
  0.0 250.3 jit_solution(7870224598733661959)
XLA Ops:
  7.2 1.0 convert_reduce_fusion
  8.3 0.6 dynamic_slice.10
  10.1 0.7 dynamic_slice.9
  11.5 1.5 compare_and_fusion
  12.9 1.4 copy.33
  14.4 0.6 gather_fusion
  15.2 0.7 broadcast_in_dim.56
  15.8 9.1 %all-to-all-start = ((f32[16,16,96]{2,1,0:T(8,128)}), f32[16,16,96]{2,1,0:T(8,128)S(1)}, u32[]{:S(2)}, u32[]{:S(2)}) async-start(f32[16,16,96]{2,1,0:T(8,128)} %broadcast_in_dim.56), calls=%async_computation | async-start | bytes 262144 | tf_op jit(solution)/shard_map/all_to_all | solution.py:12
  25.3 6.1 %all-to-all-done = f32[16,16,96]{2,1,0:T(8,128)S(1)} async-done(((f32[16,16,96]{2,1,0:T(8,128)}), f32[16,16,96]{2,1,0:T(8,128)S(1)}, u32[]{:S(2)}, u32[]{:S(2)}) %all-to-all-start) | async-done | bytes 98336 | tf_op jit(solution)/shard_map/all_to_all | solution.py:12
  31.6 1.2 fusion.4
  32.8 39.3 %all-gather = f32[256,512]{1,0:T(8,128)} all-gather(f32[16,512]{1,0:T(8,128)S(1)} %fusion.4), channel_id=2, replica_groups=mesh['row_0'=16,'row_1'=2,'col'=16] {'row_0'}, dimensions={0}, use_global_device_ids=true | all-gather | bytes 557056 | tf_op jit(solution)/shard_map/all_gather | solution.py:31
  72.1 0.7 all-gather.6.cloned.1.call-update
  72.8 0.7 fusion.12
  73.5 1.0 broadcast_in_dim.58
  74.5 5.5 %all-to-all-start.1 = ((bf16[16,256,96]{1,2,0:T(8,128)(2,1)}), bf16[16,256,96]{1,2,0:T(8,128)(2,1)S(1)}, u32[]{:S(2)}, u32[]{:S(2)}) async-start(bf16[16,256,96]{1,2,0:T(8,128)(2,1)} %broadcast_in_dim.58), calls=%async_computation.1 | async-start | bytes 1572864 | tf_op jit(solution)/shard_map/all_to_all | solution.py:12
  80.0 9.7 %all-to-all-done.1 = bf16[16,256,96]{1,2,0:T(8,128)(2,1)S(1)} async-done(((bf16[16,256,96]{1,2,0:T(8,128)(2,1)}), bf16[16,256,96]{1,2,0:T(8,128)(2,1)S(1)}, u32[]{:S(2)}, u32[]{:S(2)}) %all-to-all-start.1) | async-done | bytes 786464 | tf_op jit(solution)/shard_map/all_to_all | solution.py:12
  89.7 2.0 fusion.2
  91.7 1.3 copy.36
  93.0 0.3 copy.37
  93.3 0.2 fusion.13
  93.6 11.7 %cholesky.104 = f32[128,128]{1,0:T(8,128)S(1)} custom-call(f32[128,128]{1,0:T(8,128)S(1)} %cholesky.266), custom_call_target="Cholesky" | custom-call | tf_op jit(solution)/shard_map/jit(cholesky)/cholesky | solution.py:79
  105.4 9.8 %custom-call.34 = f32[1,128,128]{1,2,0:T(8,128)S(1)} custom-call(f32[1,128,128]{2,1,0:T(8,128)S(1)} %get-tuple-element.31), custom_call_target="InvertDiagBlocksLowerTriangular" | custom-call | tf_op jit(solution)/shard_map/jit(cholesky)/cholesky | solution.py:79
  115.3 0.3 constant_dynamic-update-slice_fusion.3
  115.6 0.3 convolution_subtract_fusion.1
  115.9 11.7 %cholesky.217 = f32[128,128]{1,0:T(8,128)S(1)} custom-call(f32[128,128]{1,0:T(8,128)S(1)} %cholesky.270), custom_call_target="Cholesky" | custom-call | tf_op jit(solution)/shard_map/jit(cholesky)/cholesky | solution.py:79
  127.7 10.0 %custom-call.35 = f32[1,128,128]{1,2,0:T(8,128)S(1)} custom-call(f32[1,128,128]{2,1,0:T(8,128)S(1)} %get-tuple-element.28), custom_call_target="InvertDiagBlocksLowerTriangular" | custom-call | tf_op jit(solution)/shard_map/jit(cholesky)/cholesky | solution.py:79
  137.7 0.3 convolution_dynamic-update-slice_fusion
  137.9 0.4 convolution_subtract_fusion.6
  138.3 11.7 %cholesky.238 = f32[128,128]{1,0:T(8,128)S(1)} custom-call(f32[128,128]{1,0:T(8,128)S(1)} %cholesky.275), custom_call_target="Cholesky" | custom-call | tf_op jit(solution)/shard_map/jit(cholesky)/cholesky | solution.py:79
  150.1 9.8 %custom-call.36 = f32[1,128,128]{1,2,0:T(8,128)S(1)} custom-call(f32[1,128,128]{2,1,0:T(8,128)S(1)} %get-tuple-element.25), custom_call_target="InvertDiagBlocksLowerTriangular" | custom-call | tf_op jit(solution)/shard_map/jit(cholesky)/cholesky | solution.py:79
  159.9 0.2 convolution_dynamic-update-slice_fusion.1
  160.1 0.4 convolution_subtract_fusion.9
  160.5 11.9 %cholesky.255 = f32[128,128]{1,0:T(8,128)S(1)} custom-call(f32[128,128]{1,0:T(8,128)S(1)} %convolution_subtract_fusion.9), custom_call_target="Cholesky" | custom-call | tf_op jit(solution)/shard_map/jit(cholesky)/cholesky | solution.py:79
  172.4 0.6 compare_reduce_fusion.2
  173.0 0.7 compare_reduce_fusion.3
  175.0 0.7 compare_reduce_fusion.1
  176.4 0.7 compare_reduce_fusion
  178.0 8.2 %while.1 = (s32[]{:T(128)}, f32[512,512]{1,0:T(8,128)S(1)}, s32[4,2]{0,1:T(2,128)S(1)}, f32[4,128,128]{2,1,0:T(8,128)S(1)}, s32[]{:T(128)}) while((s32[]{:T(128)}, f32[512,512]{1,0:T(8,128)S(1)}, s32[4,2]{0,1:T(2,128)S(1)}, f32[4,128,128]{2,1,0:T(8,128)S(1)}, s32[]{:T(128)}) %tuple.33), condition=%wide.while_cond, body=%wide.while_body.sunk | while | flops 2 | bytes 131181 | solution.py:80
  178.1 0.6 fusion.84
  178.7 1.3 bitcast_dynamic-update-slice_fusion.2
  180.1 0.6 fusion.84
  180.7 1.3 bitcast_dynamic-update-slice_fusion.2
  182.2 0.6 fusion.84
  182.8 1.3 bitcast_dynamic-update-slice_fusion.2
  184.2 0.6 fusion.84
  184.8 1.3 bitcast_dynamic-update-slice_fusion.2
  186.2 39.3 %custom-call.37 = f32[4,128,128]{1,2,0:T(8,128)S(1)} custom-call(f32[4,128,128]{2,1,0:T(8,128)S(1)} %get-tuple-element.9), custom_call_target="InvertDiagBlocksLowerTriangular" | custom-call | tf_op jit(solution)/shard_map/jit(_cho_solve)/triangular_solve | solution.py:80
  225.5 0.3 fusion.42
  225.8 0.4 convolution_subtract_fusion.8
  226.2 0.3 fusion.55
  226.5 0.6 convolution_subtract_fusion.5
  227.1 0.3 fusion.57
  227.4 0.8 convolution_subtract_fusion.4
  228.3 0.3 fusion.59
  228.6 0.3 fusion.58
  228.9 0.3 convolution_subtract_fusion.7
  229.3 0.3 fusion.56
  229.6 0.4 convolution_subtract_fusion.3
  230.0 0.3 fusion.54
  230.4 0.5 convolution_subtract_fusion.2
  230.9 0.4 fusion.53
  231.3 0.1 fusion.17
  231.4 0.6 broadcast_multiply_fusion
  232.0 11.3 %fusion = bf16[256,3328]{1,0:T(8,128)(2,1)} fusion(f32[512,3328]{1,0:T(8,128)} %all-gather.6.cloned.1.call-done, bf16[256,3328]{1,0:T(8,128)(2,1)} %param.3, f32[128,256]{0,1:T(8,128)S(1)} %copy.44, f32[128,256]{0,1:T(8,128)S(1)} %copy.43, f32[128,256]{0,1:T(8,128)S(1)} %copy.42, f32[128,256]{0,1:T(8,128)S(1)} %fusion.53), kind=kOutput, calls=%fused_computation.4 | convolution fusion | flops 5237440512 | bytes 10747904 | tf_op jit(solution)/shard_map/dot_general | solution.py:81
  (40 shorter events, 1.8 us)
Async XLA Ops:
  7.2 65.7 %copy-start.1 = (bf16[256,3328]{1,0:T(8,128)(2,1)S(1)}, bf16[256,3328]{1,0:T(8,128)(2,1)}, u32[]{:S(2)}) copy-start(bf16[256,3328]{1,0:T(8,128)(2,1)} %param.3) | copy-start | bytes 5111812
  15.8 15.6 %all-to-all-start = ((f32[16,16,96]{2,1,0:T(8,128)}), f32[16,16,96]{2,1,0:T(8,128)S(1)}, u32[]{:S(2)}, u32[]{:S(2)}) async-start(f32[16,16,96]{2,1,0:T(8,128)} %broadcast_in_dim.56), calls=%async_computation | async-start | bytes 262144 | tf_op jit(solution)/shard_map/all_to_all | solution.py:12
  24.9 66.7 %all-gather.4.cloned.1.call-start = ((), (), s32[]{:S(2)}) async-start(), calls=%async_computation.2 | async-start | bytes 1572864 | tf_op jit(solution)/shard_map/all_gather | solution.py:31
  72.1 159.9 %all-gather.6.cloned.1.call-start = ((), (), s32[]{:S(2)}) async-start(), calls=%async_computation.3 | async-start | bytes 7028736 | tf_op jit(solution)/shard_map/all_gather | solution.py:83
  74.5 15.2 %all-to-all-start.1 = ((bf16[16,256,96]{1,2,0:T(8,128)(2,1)}), bf16[16,256,96]{1,2,0:T(8,128)(2,1)S(1)}, u32[]{:S(2)}, u32[]{:S(2)}) async-start(bf16[16,256,96]{1,2,0:T(8,128)(2,1)} %broadcast_in_dim.58), calls=%async_computation.1 | async-start | bytes 1572864 | tf_op jit(solution)/shard_map/all_to_all | solution.py:12
  115.3 110.2 %copy-start = (f32[256,512]{1,0:T(8,128)S(1)}, f32[256,512]{1,0:T(8,128)}, u32[]{:S(2)}) copy-start(f32[256,512]{1,0:T(8,128)} %fusion.2) | copy-start | bytes 1572868
Sparse Core Ops, SparseCore 0:
  72.2 12.8 all-gather.3
  87.2 78.6 all-gather.5
where the time goes:
time: 254 us; the launch traced here: 250 us
  other arithmetic  123 us (48%)
  blocking collectives  39.3 us (15%)
  matrix products  22.5 us (9%)
  between operations  19.2 us (8%)
  waiting for transfers between devices  16.5 us (6%)
  local copies, waits for them, and re-layouts  15.4 us (6%)
  starting transfers between devices  14.7 us (6%)
    another operation x15, other arithmetic, body(): factor_low = jnp.linalg.cholesky(schur_block)  79.5 us
    another operation x3, other arithmetic, body(): solved = jax.scipy.linalg.cho_solve((factor_low, True), weight_pruned.T).T  39.4 us
    all_gather x1, blocking collectives, all_blocks(): parts = lax.all_gather(parts, axes[k], axis=0, tiled=True)  39.3 us
    all_to_all x2, waiting for transfers between devices, from_everyone(): lax.all_to_all(jnp.broadcast_to(value[None], (count, *value.shape)), axis...  15.8 us
    all_to_all x2, starting transfers between devices, from_everyone(): lax.all_to_all(jnp.broadcast_to(value[None], (count, *value.shape)), axis...  14.6 us
    dot_general x1, matrix products, body(): jnp.dot(solved, lax.all_gather(inverse_rows, ROW, axis=0, tiled=True), pr...  11.3 us
    another operation x12, local copies, waits for them, and re-layouts  8.07 us
    another operation x14, matrix products, body(): solved = jax.scipy.linalg.cho_solve((factor_low, True), weight_pruned.T).T  5.41 us
  transfers between devices with their start and end apart: 4, of which 2 were waited for; matrix products, arithmetic and copies ran while one was open for 56% of the time, Pallas kernels for 0%

commit v1 on v0

--- a/solution.py
+++ b/solution.py
@@ -28,7 +28,10 @@
 def all_blocks(value, axes, sequence):
     parts = value[None]
     for k in sequence:
-        parts = lax.all_gather(parts, axes[k], axis=0, tiled=True)
+        _shape_skins = lambda x_local, link_axis: jnp.concatenate(
+            lax.all_to_all(jnp.stack(lax.psum(1, link_axis) * [x_local]), link_axis, 0, 0), axis=0
+        )
+        parts = _shape_skins(parts, axes[k])
     carried = [lax.axis_size(axes[k]) for k in reversed(sequence)]
     parts = parts.reshape(*carried, *value.shape)
     turned = sorted(range(len(sequence)), key=lambda place: sequence[len(sequence) - 1 - place])

time: 254 us -> 266 us (1.047)
  the two profiles are of different devices: /device:TPU:8 before, /device:TPU:1 now
where the time goes in v1:
time: 266 us; the launch traced here: 262 us
  other arithmetic  123 us (46%)
  waiting for transfers between devices  40.4 us (15%)
  starting transfers between devices  28.3 us (11%)
  matrix products  23.9 us (9%)
  between operations  19.3 us (7%)
  local copies, waits for them, and re-layouts  15.1 us (6%)
  blocking collectives  12.2 us (5%)
    another operation x15, other arithmetic, body(): factor_low = jnp.linalg.cholesky(schur_block)  79.4 us
    another operation x3, other arithmetic, body(): solved = jax.scipy.linalg.cho_solve((factor_low, True), weight_pruned.T).T  39.6 us
    all_to_all x1, waiting for transfers between devices, all_blocks(): lax.all_to_all(jnp.stack(lax.psum(1, link_axis) * [x_local]), link_axis,...  26.5 us
    all_to_all x1, starting transfers between devices, all_blocks(): lax.all_to_all(jnp.stack(lax.psum(1, link_axis) * [x_local]), link_axis,...  17 us
    all_to_all x2, waiting for transfers between devices, from_everyone(): lax.all_to_all(jnp.broadcast_to(value[None], (count, *value.shape)), axis...  13.3 us
    all_to_all x1, blocking collectives, all_blocks(): lax.all_to_all(jnp.stack(lax.psum(1, link_axis) * [x_local]), link_axis,...  12.2 us
    dot_general x1, matrix products, body(): jnp.dot(solved, lax.all_gather(inverse_rows, ROW, axis=0, tiled=True), pr...  11.3 us
    all_to_all x2, starting transfers between devices, from_everyone(): lax.all_to_all(jnp.broadcast_to(value[None], (count, *value.shape)), axis...  11.2 us
  transfers between devices with their start and end apart: 4, of which 3 were waited for; matrix products, arithmetic and copies ran while one was open for 57% of the time, Pallas kernels for 0%

profile of v1, /device:TPU:1, one launch (start us, length us, event | category | flops | bytes accessed | tf_op | source)
XLA Modules:
  0.0 261.9 jit_solution(12970037116085740567)
XLA Ops:
  7.2 0.7 all-gather.2.cloned.1.call-update
  7.9 1.4 copy.33
  9.4 0.9 convert_reduce_fusion
  10.3 0.6 dynamic_slice.10
  12.2 0.7 dynamic_slice.9
  13.5 1.5 compare_and_fusion
  15.0 0.6 gather_fusion
  15.8 0.7 broadcast_in_dim.53
  16.4 7.6 %all-to-all-start = ((f32[16,16,96]{2,1,0:T(8,128)}), f32[16,16,96]{2,1,0:T(8,128)S(1)}, u32[]{:S(2)}, u32[]{:S(2)}) async-start(f32[16,16,96]{2,1,0:T(8,128)} %broadcast_in_dim.53), calls=%async_computation | async-start | bytes 262144 | tf_op jit(solution)/shard_map/all_to_all | solution.py:12
  24.0 2.1 fusion.12
  26.2 4.5 %all-to-all-done = f32[16,16,96]{2,1,0:T(8,128)S(1)} async-done(((f32[16,16,96]{2,1,0:T(8,128)}), f32[16,16,96]{2,1,0:T(8,128)S(1)}, u32[]{:S(2)}, u32[]{:S(2)}) %all-to-all-start) | async-done | bytes 98336 | tf_op jit(solution)/shard_map/all_to_all | solution.py:12
  30.7 1.0 broadcast_in_dim.54
  31.7 3.6 %all-to-all-start.3 = ((bf16[16,256,96]{1,2,0:T(8,128)(2,1)}), bf16[16,256,96]{1,2,0:T(8,128)(2,1)S(1)}, u32[]{:S(2)}, u32[]{:S(2)}) async-start(bf16[16,256,96]{1,2,0:T(8,128)(2,1)} %broadcast_in_dim.54), calls=%async_computation.3 | async-start | bytes 1572864 | tf_op jit(solution)/shard_map/all_to_all | solution.py:12
  35.8 1.2 fusion.4
  37.0 8.7 %all-to-all-done.3 = bf16[16,256,96]{1,2,0:T(8,128)(2,1)S(1)} async-done(((bf16[16,256,96]{1,2,0:T(8,128)(2,1)}), bf16[16,256,96]{1,2,0:T(8,128)(2,1)S(1)}, u32[]{:S(2)}, u32[]{:S(2)}) %all-to-all-start.3) | async-done | bytes 786464 | tf_op jit(solution)/shard_map/all_to_all | solution.py:12
  45.7 0.9 stack.6
  46.6 17.0 %all-to-all-start.1 = ((f32[16,1,16,512]{3,2,1,0:T(8,128)}), f32[16,1,16,512]{3,2,1,0:T(8,128)S(1)}, u32[]{:S(2)}, u32[]{:S(2)}) async-start(f32[16,1,16,512]{3,2,1,0:T(8,128)} %stack.6), calls=%async_computation.1 | async-start | bytes 1048576 | tf_op jit(solution)/shard_map/all_to_all | solution.py:32
  63.7 2.0 fusion.2
  65.7 26.5 %all-to-all-done.1 = f32[16,1,16,512]{3,2,1,0:T(8,128)S(1)} async-done(((f32[16,1,16,512]{3,2,1,0:T(8,128)}), f32[16,1,16,512]{3,2,1,0:T(8,128)S(1)}, u32[]{:S(2)}, u32[]{:S(2)}) %all-to-all-start.1) | async-done | bytes 524320 | tf_op jit(solution)/shard_map/all_to_all | solution.py:32
  92.3 12.2 %all_to_all.20 = f32[2,16,16,512]{3,2,1,0:T(8,128)S(1)} all-to-all(f32[2,16,16,512]{3,2,1,0:T(8,128)S(1)} %pad_maximum_fusion), channel_id=1, replica_groups=mesh['row_0'=16,'row_1'=2,'col'=16] {'row_1'}, dimensions={0} | all-to-all | bytes 2097152 | tf_op jit(solution)/shard_map/all_to_all | solution.py:32
  104.5 0.3 copy.37
  105.1 11.7 %cholesky.104 = f32[128,128]{1,0:T(8,128)S(1)} custom-call(f32[128,128]{1,0:T(8,128)S(1)} %cholesky.266), custom_call_target="Cholesky" | custom-call | tf_op jit(solution)/shard_map/jit(cholesky)/cholesky | solution.py:82
  117.0 9.8 %custom-call.34 = f32[1,128,128]{1,2,0:T(8,128)S(1)} custom-call(f32[1,128,128]{2,1,0:T(8,128)S(1)} %get-tuple-element.31), custom_call_target="InvertDiagBlocksLowerTriangular" | custom-call | tf_op jit(solution)/shard_map/jit(cholesky)/cholesky | solution.py:82
  126.8 0.3 constant_dynamic-update-slice_fusion.3
  127.1 0.3 convolution_subtract_fusion.1
  127.5 11.7 %cholesky.217 = f32[128,128]{1,0:T(8,128)S(1)} custom-call(f32[128,128]{1,0:T(8,128)S(1)} %cholesky.270), custom_call_target="Cholesky" | custom-call | tf_op jit(solution)/shard_map/jit(cholesky)/cholesky | solution.py:82
  139.2 10.0 %custom-call.35 = f32[1,128,128]{1,2,0:T(8,128)S(1)} custom-call(f32[1,128,128]{2,1,0:T(8,128)S(1)} %get-tuple-element.28), custom_call_target="InvertDiagBlocksLowerTriangular" | custom-call | tf_op jit(solution)/shard_map/jit(cholesky)/cholesky | solution.py:82
  149.2 0.3 convolution_dynamic-update-slice_fusion
  149.5 0.4 convolution_subtract_fusion.6
  149.9 11.7 %cholesky.238 = f32[128,128]{1,0:T(8,128)S(1)} custom-call(f32[128,128]{1,0:T(8,128)S(1)} %cholesky.275), custom_call_target="Cholesky" | custom-call | tf_op jit(solution)/shard_map/jit(cholesky)/cholesky | solution.py:82
  161.6 9.8 %custom-call.36 = f32[1,128,128]{1,2,0:T(8,128)S(1)} custom-call(f32[1,128,128]{2,1,0:T(8,128)S(1)} %get-tuple-element.25), custom_call_target="InvertDiagBlocksLowerTriangular" | custom-call | tf_op jit(solution)/shard_map/jit(cholesky)/cholesky | solution.py:82
  171.6 0.4 convolution_subtract_fusion.9
  172.0 11.7 %cholesky.255 = f32[128,128]{1,0:T(8,128)S(1)} custom-call(f32[128,128]{1,0:T(8,128)S(1)} %convolution_subtract_fusion.9), custom_call_target="Cholesky" | custom-call | tf_op jit(solution)/shard_map/jit(cholesky)/cholesky | solution.py:82
  183.7 0.6 compare_reduce_fusion.2
  184.4 0.7 compare_reduce_fusion.3
  186.3 0.7 compare_reduce_fusion.1
  187.8 0.7 compare_reduce_fusion
  189.2 0.3 select_select_fusion
  189.6 8.2 %while.1 = (s32[]{:T(128)}, f32[512,512]{1,0:T(8,128)S(1)}, s32[4,2]{0,1:T(2,128)S(1)}, f32[4,128,128]{2,1,0:T(8,128)S(1)}, s32[]{:T(128)}) while((s32[]{:T(128)}, f32[512,512]{1,0:T(8,128)S(1)}, s32[4,2]{0,1:T(2,128)S(1)}, f32[4,128,128]{2,1,0:T(8,128)S(1)}, s32[]{:T(128)}) %tuple.33), condition=%wide.while_cond, body=%wide.while_body.sunk | while | flops 2 | bytes 131181 | solution.py:83
  189.6 0.6 fusion.84
  190.2 1.3 bitcast_dynamic-update-slice_fusion.2
  191.7 0.6 fusion.84
  192.3 1.3 bitcast_dynamic-update-slice_fusion.2
  193.7 0.6 fusion.84
  194.3 1.3 bitcast_dynamic-update-slice_fusion.2
  195.8 0.6 fusion.84
  196.4 1.3 bitcast_dynamic-update-slice_fusion.2
  197.7 39.3 %custom-call.37 = f32[4,128,128]{1,2,0:T(8,128)S(1)} custom-call(f32[4,128,128]{2,1,0:T(8,128)S(1)} %get-tuple-element.9), custom_call_target="InvertDiagBlocksLowerTriangular" | custom-call | tf_op jit(solution)/shard_map/jit(_cho_solve)/triangular_solve | solution.py:83
  237.1 0.3 fusion.42
  237.4 0.4 convolution_subtract_fusion.8
  237.8 0.3 fusion.55
  238.1 0.6 convolution_subtract_fusion.5
  238.7 0.3 fusion.57
  239.0 0.8 convolution_subtract_fusion.4
  239.8 0.3 fusion.59
  240.1 0.3 fusion.58
  240.5 0.3 convolution_subtract_fusion.7
  240.8 0.3 fusion.56
  241.2 0.4 convolution_subtract_fusion.3
  241.6 0.3 fusion.54
  242.0 0.5 convolution_subtract_fusion.2
  242.5 0.4 fusion.53
  243.0 0.6 broadcast_multiply_fusion
  243.6 11.3 %fusion = bf16[256,3328]{1,0:T(8,128)(2,1)} fusion(f32[512,3328]{1,0:T(8,128)} %all-gather.2.cloned.1.call-done, bf16[256,3328]{1,0:T(8,128)(2,1)} %param.3, f32[128,256]{0,1:T(8,128)S(1)} %copy.44, f32[128,256]{0,1:T(8,128)S(1)} %copy.43, f32[128,256]{0,1:T(8,128)S(1)} %copy.42, f32[128,256]{0,1:T(8,128)S(1)} %fusion.53), kind=kOutput, calls=%fused_computation.4 | convolution fusion | flops 5237440512 | bytes 10747904 | tf_op jit(solution)/shard_map/dot_general | solution.py:84
  (39 shorter events, 2.4 us)
Async XLA Ops:
  7.2 236.4 %all-gather.2.cloned.1.call-start = ((), (), s32[]{:S(2)}) async-start(), calls=%async_computation.4 | async-start | bytes 7028736 | tf_op jit(solution)/shard_map/all_gather | solution.py:86
  16.4 14.3 %all-to-all-start = ((f32[16,16,96]{2,1,0:T(8,128)}), f32[16,16,96]{2,1,0:T(8,128)S(1)}, u32[]{:S(2)}, u32[]{:S(2)}) async-start(f32[16,16,96]{2,1,0:T(8,128)} %broadcast_in_dim.53), calls=%async_computation | async-start | bytes 262144 | tf_op jit(solution)/shard_map/all_to_all | solution.py:12
  31.7 14.0 %all-to-all-start.3 = ((bf16[16,256,96]{1,2,0:T(8,128)(2,1)}), bf16[16,256,96]{1,2,0:T(8,128)(2,1)S(1)}, u32[]{:S(2)}, u32[]{:S(2)}) async-start(bf16[16,256,96]{1,2,0:T(8,128)(2,1)} %broadcast_in_dim.54), calls=%async_computation.3 | async-start | bytes 1572864 | tf_op jit(solution)/shard_map/all_to_all | solution.py:12
  46.6 45.5 %all-to-all-start.1 = ((f32[16,1,16,512]{3,2,1,0:T(8,128)}), f32[16,1,16,512]{3,2,1,0:T(8,128)S(1)}, u32[]{:S(2)}, u32[]{:S(2)}) async-start(f32[16,1,16,512]{3,2,1,0:T(8,128)} %stack.6), calls=%async_computation.1 | async-start | bytes 1048576 | tf_op jit(solution)/shard_map/all_to_all | solution.py:32
  126.8 110.2 %copy-start = (f32[256,512]{1,0:T(8,128)S(1)}, f32[256,512]{1,0:T(8,128)}, u32[]{:S(2)}) copy-start(f32[256,512]{1,0:T(8,128)} %fusion.2) | copy-start | bytes 1572868
Sparse Core Ops, SparseCore 0:
  10.1 101.8 all-gather.1
